TPU v7x, 512 devices: a whole 4x8x8 slice. The times are simulated.
512 devices in a mesh: pair: 32 (over y, x), row: 16 (over z, core).
Axes of the slice: x: 4, y: 8, z: 8, core: 2. Of those that a mesh axis runs over, the one named last changes fastest.
Arguments:
- r_factor: float32 [16384, 16384], P(('row', 'pair')), may hold values from -40 to 40, as said below
- block_slots: int32 [256], replicated, may hold values from 0 to 255, as said below
Outputs:
- rotated: float32 [16384, 16384], P('row', 'pair')
- off_ratio: float32 [], replicated
Inputs may be any that keep to these rules, and one draw needn't show every extreme that they name: `block_slots`: each of the 256 column blocks appears exactly once. `r_factor`: entries below the diagonal are zero and the diagonal is positive.
All inputs are finite; a program needn't handle non-finite values.
Results may differ from a plain program's by a relative error of at most 0.0001.
Values sent between devices are 32-bit elements; how exact they have to be, the bound alone decides.
A program may use at most 64 MiB of HBM per device.

v0:
```python
import jax
import jax.numpy as jnp
from jax import lax
from jax.sharding import PartitionSpec as P

BLOCK = 64
ITERS = 3


def passed_along(value, axis, by):
    count = lax.axis_size(axis)
    pairs = [(i, i + by) for i in range(count) if 0 <= i + by < count]
    return lax.ppermute(value, axis, pairs)


def cayley(pair_gram):
    size_n = pair_gram.shape[0]
    diag_vals = jnp.diagonal(pair_gram)
    spread = diag_vals[:, None] - diag_vals[None, :]
    denom = 2.0 * (diag_vals[:, None] ** 2 + diag_vals[None, :] ** 2)
    skew_part = pair_gram * spread / denom
    unit_matrix = jnp.eye(size_n, dtype=pair_gram.dtype)
    minus_part = unit_matrix - skew_part
    system = unit_matrix - jnp.dot(skew_part, skew_part, precision=lax.Precision.HIGHEST)
    product = jnp.dot(minus_part, minus_part, precision=lax.Precision.HIGHEST)
    factor = jnp.linalg.cholesky(system)
    return jax.scipy.linalg.cho_solve((factor, True), product.T).T


def square_sums(rows_part):
    row_ids = jnp.arange(rows_part.shape[1], dtype=jnp.int32)[:, None]
    col_ids = jnp.arange(rows_part.shape[2], dtype=jnp.int32)[None, :]
    on_diag = (row_ids == col_ids)[None, :, :]
    squares = rows_part * rows_part
    return (jnp.sum(jnp.where(on_diag, 0.0, squares)), jnp.sum(jnp.where(on_diag, squares, 0.0)))


def on_device(r_factor, block_slots):
    rows_in, total_cols = r_factor.shape
    blocks = total_cols // BLOCK
    pair_width = 2 * BLOCK
    arranged = jnp.take(r_factor.reshape(rows_in, blocks, BLOCK), block_slots, axis=1)
    arranged = arranged.reshape(rows_in, blocks // 2, pair_width)
    received = lax.all_to_all(arranged, "pair", split_axis=1, concat_axis=0, tiled=True)
    column = jnp.transpose(received, (1, 0, 2))
    local_pairs = column.shape[0]
    rows_here = column.shape[1]
    totals = None
    for sweep in range(ITERS):
        partial_value = jnp.einsum("pri,prj->pij", column, column, precision=lax.Precision.HIGHEST)
        pair_gram = lax.psum(partial_value, "row")
        if sweep == 0:
            off_part, diag_part = square_sums(pair_gram)
            totals = lax.psum((off_part, diag_part), "pair")
        rotation = jax.vmap(cayley)(pair_gram)
        column = jnp.einsum("pri,pij->prj", column, rotation, precision=lax.Precision.HIGHEST)
    upper_half = column[:, :, :BLOCK]
    lower_half = column[:, :, BLOCK:]
    pair_index = lax.axis_index("pair")
    pair_count = lax.axis_size("pair")
    global_ids = pair_index * local_pairs + jnp.arange(local_pairs, dtype=jnp.int32)
    last_id = pair_count * local_pairs - 1
    first_mask = (global_ids == 0)[:, None, None]
    last_mask = (global_ids == last_id)[:, None, None]
    forward = jnp.where(first_mask, lower_half, upper_half)
    came_up = passed_along(forward[local_pairs - 1], "pair", 1)
    came_down = passed_along(lower_half[0], "pair", -1)
    before = jnp.concatenate([came_up[None], forward[: local_pairs - 1]], axis=0)
    after = jnp.concatenate([lower_half[1:], came_down[None]], axis=0)
    new_upper = jnp.where(first_mask, upper_half, before)
    new_lower = jnp.where(last_mask, upper_half, after)
    joined = jnp.concatenate([new_upper, new_lower], axis=2)
    rotated = jnp.transpose(joined, (1, 0, 2)).reshape(rows_here, local_pairs * pair_width)
    off_ratio = jnp.sqrt(totals[0] / totals[1])
    return (rotated, off_ratio)


def solution(mesh):
    in_specs = (P(("row", "pair"), None), P())
    out_specs = (P("row", "pair"), P())
    return jax.shard_map(
        on_device, mesh=mesh, in_specs=in_specs, out_specs=out_specs, check_vma=False
    )
```

profile of v0, /device:TPU:32, one launch (start us, length us, event | category | flops | bytes accessed | tf_op | source)
XLA Modules:
  0.0 870.0 jit_solution(1644041194459896223)
XLA Ops:
  8.9 4.3 reshape.87
  13.2 6.5 copy.172
  19.7 5.0 gather_fusion
  24.7 6.5 copy.173
  37.3 9.8 %all-to-all-start = ((f32[32,128,128]{2,0,1:T(8,128)}), f32[32,128,128]{2,0,1:T(8,128)S(1)}, u32[]{:S(2)}, u32[]{:S(2)}) async-start(f32[32,128,128]{2,0,1:T(8,128)} %copy.174), calls=%async_computation | async-start | bytes 4194304 | tf_op jit(solution)/shard_map/all_to_all | solution.py:44
  47.4 46.9 %all-to-all-done = f32[32,128,128]{2,0,1:T(8,128)S(1)} async-done(((f32[32,128,128]{2,0,1:T(8,128)}), f32[32,128,128]{2,0,1:T(8,128)S(1)}, u32[]{:S(2)}, u32[]{:S(2)}) %all-to-all-start) | async-done | bytes 2097184 | tf_op jit(solution)/shard_map/all_to_all | solution.py:44
  97.4 4.3 fusion.33
  101.8 119.5 %all-reduce.5.cloned.1.call-done = f32[4,128,128]{1,2,0:T(8,128)} async-done(((f32[4,128,128]{1,2,0:T(8,128)}), f32[4,128,128]{1,2,0:T(8,128)}) %all-reduce.5.cloned.1.call-update) | async-done | bytes 262160 | tf_op jit(solution)/shard_map/psum | solution.py:51
  221.3 8.5 copy.178
  232.4 46.9 %custom-call.18 = f32[4,128,128]{2,1,0:T(8,128)S(1)} custom-call(f32[4,128,128]{2,1,0:T(8,128)S(1)} %fusion.14), custom_call_target="Cholesky" | custom-call | tf_op jit(solution)/shard_map/vmap(jit(cholesky))/cholesky | solution.py:26
  279.6 39.7 %custom-call.19 = f32[4,1,128,128]{2,3,1,0:T(8,128)S(1)} custom-call(f32[4,1,128,128]{3,2,1,0:T(8,128)S(1)} %select_bitcast_fusion.2), custom_call_target="InvertDiagBlocksLowerTriangular" | custom-call | tf_op jit(solution)/shard_map/vmap(jit(_cho_solve))/triangular_solve | solution.py:27
  324.3 4.3 fusion.35
  328.6 116.2 %all-reduce.7.cloned.1.call-done = f32[4,128,128]{1,2,0:T(8,128)} async-done(((f32[4,128,128]{1,2,0:T(8,128)}), f32[4,128,128]{1,2,0:T(8,128)}) %all-reduce.7.cloned.1.call-update) | async-done | bytes 262160 | tf_op jit(solution)/shard_map/psum | solution.py:51
  444.8 8.5 copy.188
  456.0 46.9 %custom-call.20 = f32[4,128,128]{2,1,0:T(8,128)S(1)} custom-call(f32[4,128,128]{2,1,0:T(8,128)S(1)} %fusion.9), custom_call_target="Cholesky" | custom-call | tf_op jit(solution)/shard_map/vmap(jit(cholesky))/cholesky | solution.py:26
  503.2 39.5 %custom-call.21 = f32[4,1,128,128]{2,3,1,0:T(8,128)S(1)} custom-call(f32[4,1,128,128]{3,2,1,0:T(8,128)S(1)} %select_bitcast_fusion.1), custom_call_target="InvertDiagBlocksLowerTriangular" | custom-call | tf_op jit(solution)/shard_map/vmap(jit(_cho_solve))/triangular_solve | solution.py:27
  544.4 3.5 fusion.36
  547.9 4.3 fusion.37
  552.2 116.0 %all-reduce.9.cloned.1.call-done = f32[4,128,128]{1,2,0:T(8,128)} async-done(((f32[4,128,128]{1,2,0:T(8,128)}), f32[4,128,128]{1,2,0:T(8,128)}) %all-reduce.9.cloned.1.call-update) | async-done | bytes 262160 | tf_op jit(solution)/shard_map/psum | solution.py:51
  668.3 8.5 copy.198
  680.1 47.9 %custom-call.22 = f32[4,128,128]{2,1,0:T(8,128)S(1)} custom-call(f32[4,128,128]{2,1,0:T(8,128)} %fusion.4), custom_call_target="Cholesky" | custom-call | tf_op jit(solution)/shard_map/vmap(jit(cholesky))/cholesky | solution.py:26
  728.3 39.3 %custom-call.23 = f32[4,1,128,128]{2,3,1,0:T(8,128)S(1)} custom-call(f32[4,1,128,128]{3,2,1,0:T(8,128)S(1)} %select_bitcast_fusion), custom_call_target="InvertDiagBlocksLowerTriangular" | custom-call | tf_op jit(solution)/shard_map/vmap(jit(_cho_solve))/triangular_solve | solution.py:27
  772.1 4.6 collective-permute-start.1
  780.4 75.6 %all-reduce = (f32[]{:T(128)}, f32[]{:T(128)}) all-reduce(f32[]{:T(128)} %get-tuple-element.15, f32[]{:T(128)} %get-tuple-element.14), channel_id=1, replica_groups=mesh['pair'=32,'row'=16] {'pair'}, use_global_device_ids=true, to_apply=%region_6.9 | all-reduce | flops 2 | bytes 16 | tf_op jit(solution)/shard_map/psum | solution.py:54
  (88 shorter events, 40.1 us)
Async XLA Ops:
  37.3 57.0 %all-to-all-start = ((f32[32,128,128]{2,0,1:T(8,128)}), f32[32,128,128]{2,0,1:T(8,128)S(1)}, u32[]{:S(2)}, u32[]{:S(2)}) async-start(f32[32,128,128]{2,0,1:T(8,128)} %copy.174), calls=%async_computation | async-start | bytes 4194304 | tf_op jit(solution)/shard_map/all_to_all | solution.py:44
  47.1 174.2 %all-reduce.5.cloned.1.call-start = ((), (), s32[]{:S(2)}) async-start(), calls=%async_computation.1 | async-start | bytes 524288 | tf_op jit(solution)/shard_map/psum | solution.py:51
  94.3 1.3 copy-start.3
  101.7 343.1 %all-reduce.7.cloned.1.call-start = ((), (), s32[]{:S(2)}) async-start(), calls=%async_computation.2 | async-start | bytes 524288 | tf_op jit(solution)/shard_map/psum | solution.py:51
  221.3 10.3 %copy-start.4 = (f32[4,128,128]{1,2,0:T(8,128)S(1)}, f32[4,128,128]{1,2,0:T(8,128)}, u32[]{:S(2)}) copy-start(f32[4,128,128]{1,2,0:T(8,128)} %all-reduce.5.cloned.1.call-done) | copy-start | bytes 786436
  323.0 1.3 copy-start
  328.6 339.7 %all-reduce.9.cloned.1.call-start = ((), (), s32[]{:S(2)}) async-start(), calls=%async_computation.3 | async-start | bytes 524288 | tf_op jit(solution)/shard_map/psum | solution.py:51
  444.8 10.4 %copy-start.6 = (f32[4,128,128]{1,2,0:T(8,128)S(1)}, f32[4,128,128]{1,2,0:T(8,128)}, u32[]{:S(2)}) copy-start(f32[4,128,128]{1,2,0:T(8,128)} %all-reduce.7.cloned.1.call-done) | copy-start | bytes 786436
  668.3 10.3 %copy-start.5 = (f32[4,128,128]{1,2,0:T(8,128)S(1)}, f32[4,128,128]{1,2,0:T(8,128)}, u32[]{:S(2)}) copy-start(f32[4,128,128]{1,2,0:T(8,128)} %all-reduce.9.cloned.1.call-done) | copy-start | bytes 786436
  771.3 6.3 copy-start.1
  772.1 86.4 %collective-permute-start.1 = (f32[1024,64]{0,1:T(8,128)}, f32[1024,64]{0,1:T(8,128)}, u32[]{:S(2)}, u32[]{:S(2)}) collective-permute-start(f32[1024,64]{0,1:T(8,128)} %slice_bitcast_fusion), channel_id=1, source_target_pairs={{16,0},{32,16},{48,32},{64,48},{80,64},{96,80},{112,96},{128,112},... | collective-permute-start | bytes 786440 | tf_op jit(solution)/shard_map/ppermute | solution.py:13
  777.6 80.9 %collective-permute-start = (f32[1024,64]{0,1:T(8,128)}, f32[1024,64]{0,1:T(8,128)}, u32[]{:S(2)}, u32[]{:S(2)}) collective-permute-start(f32[1024,64]{0,1:T(8,128)} %slice_bitcast_fusion.1), channel_id=1, source_target_pairs={{0,16},{16,32},{32,48},{48,64},{64,80},{80,96},{96,112},{112,128},... | collective-permute-start | bytes 786440 | tf_op jit(solution)/shard_map/ppermute | solution.py:13
  779.5 79.0 %copy-start.2 = (f32[4,1024,128]{1,2,0:T(8,128)S(1)}, f32[4,1024,128]{1,2,0:T(8,128)}, u32[]{:S(2)}) copy-start(f32[4,1024,128]{1,2,0:T(8,128)} %copy-done.1) | copy-start | bytes 6291460
Sparse Core Ops, SparseCore 0:
  101.8 119.4 all-reduce.4
  328.7 116.0 all-reduce.6
  552.3 115.8 all-reduce.8
where the time goes:
time: 877 us; the launch traced here: 870 us
  waiting for transfers between devices  399 us (45%)
  other arithmetic  266 us (30%)
  blocking collectives  75.6 us (9%)
  local copies, waits for them, and re-layouts  68.9 us (8%)
  matrix products  27.1 us (3%)
  between operations  17 us (2%)
  starting transfers between devices  16.6 us (2%)
    psum x3, waiting for transfers between devices, on_device(): pair_gram = lax.psum(partial_value, 'row')  352 us
    another operation x10, other arithmetic, cayley(): factor = jnp.linalg.cholesky(system)  142 us
    another operation x7, other arithmetic, cayley(): return jax.scipy.linalg.cho_solve((factor, True), product.T).T  119 us
    psum x1, blocking collectives, on_device(): totals = lax.psum((off_part, diag_part), 'pair')  75.6 us
    all_to_all x1, waiting for transfers between devices, on_device(): lax.all_to_all(arranged, 'pair', split_axis=1, concat_axis=0, tiled=True)  46.9 us
    psum x3, local copies, waits for them, and re-layouts, on_device(): pair_gram = lax.psum(partial_value, 'row')  25.4 us
  transfers between devices with their start and end apart: 6, of which 4 were waited for; matrix products, arithmetic and copies ran while one was open for 0% of the time, Pallas kernels for 0%

commit v1 on v0

--- a/solution.py
+++ b/solution.py
@@ -48,7 +48,11 @@
     totals = None
     for sweep in range(ITERS):
         partial_value = jnp.einsum("pri,prj->pij", column, column, precision=lax.Precision.HIGHEST)
-        pair_gram = lax.psum(partial_value, "row")
+        pair_gram = partial_value
+        for hop in (1, 2, 4, 8):
+            pair_gram = pair_gram + lax.ppermute(
+                pair_gram, "row", [(dev, dev ^ hop) for dev in range(16)]
+            )
         if sweep == 0:
             off_part, diag_part = square_sums(pair_gram)
             totals = lax.psum((off_part, diag_part), "pair")

time: 877 us -> 652 us (0.74)
  waiting for transfers between devices: 399 us -> 101 us
  blocking collectives: 75.6 us -> 131 us
  starting transfers between devices: 16.6 us -> 57.5 us
  between operations: 17 us -> 4.18 us
    psum x3 -> x0, waiting for transfers between devices: 352 us -> none  [on_device(): pair_gram = lax.psum(partial_value, 'row')]
    ppermute x0 -> x12, waiting for transfers between devices: none -> 101 us  [on_device(): lax.ppermute(pair_gram, 'row', [(dev, dev ^ hop) for dev in range(16)])]
    all_to_all x0 -> x1, blocking collectives: none -> 57.5 us  [on_device(): lax.all_to_all(arranged, 'pair', split_axis=1, concat_axis=0, tiled=True)]
    ppermute x0 -> x12, starting transfers between devices: none -> 48.2 us  [on_device(): lax.ppermute(pair_gram, 'row', [(dev, dev ^ hop) for dev in range(16)])]
    all_to_all x1 -> x0, waiting for transfers between devices: 46.9 us -> none  [on_device(): lax.all_to_all(arranged, 'pair', split_axis=1, concat_axis=0, tiled=True)]
    psum x3 -> x0, local copies, waits for them, and re-layouts: 25.4 us -> none  [on_device(): pair_gram = lax.psum(partial_value, 'row')]
    add x0 -> x3, local copies, waits for them, and re-layouts: none -> 23.1 us  [on_device(): pair_gram + lax.ppermute(pair_gram, 'row', [(dev, dev ^ hop) for dev in r...]
    all_to_all x1 -> x0, starting transfers between devices: 9.83 us -> none  [on_device(): lax.all_to_all(arranged, 'pair', split_axis=1, concat_axis=0, tiled=True)]
  transfers between devices with their start and end apart: 6 -> 14, of which waited for: 4 -> 12; matrix products, arithmetic and copies ran while one was open for 0% -> 0% of each run, Pallas kernels for 0% -> 0%
where the time goes in v1:
time: 652 us; the launch traced here: 644 us
  other arithmetic  265 us (41%)
  blocking collectives  131 us (20%)
  waiting for transfers between devices  101 us (15%)
  local copies, waits for them, and re-layouts  60.9 us (9%)
  starting transfers between devices  57.5 us (9%)
  matrix products  25.1 us (4%)
    another operation x10, other arithmetic, cayley(): factor = jnp.linalg.cholesky(system)  141 us
    another operation x7, other arithmetic, cayley(): return jax.scipy.linalg.cho_solve((factor, True), product.T).T  119 us
    ppermute x12, waiting for transfers between devices, on_device(): lax.ppermute(pair_gram, 'row', [(dev, dev ^ hop) for dev in range(16)])  101 us
    psum x1, blocking collectives, on_device(): totals = lax.psum((off_part, diag_part), 'pair')  73.5 us
    all_to_all x1, blocking collectives, on_device(): lax.all_to_all(arranged, 'pair', split_axis=1, concat_axis=0, tiled=True)  57.5 us
    ppermute x12, starting transfers between devices, on_device(): lax.ppermute(pair_gram, 'row', [(dev, dev ^ hop) for dev in range(16)])  48.2 us
    add x3, local copies, waits for them, and re-layouts, on_device(): pair_gram + lax.ppermute(pair_gram, 'row', [(dev, dev ^ hop) for dev in r...  23.1 us
    gather x3, local copies, waits for them, and re-layouts, on_device(): jnp.take(r_factor.reshape(rows_in, blocks, BLOCK), block_slots, axis=1)  14.8 us
  transfers between devices with their start and end apart: 14, of which 12 were waited for; matrix products, arithmetic and copies ran while one was open for 0% of the time, Pallas kernels for 0%

profile of v1, /device:TPU:32, one launch (start us, length us, event | category | flops | bytes accessed | tf_op | source)
XLA Modules:
  0.0 644.2 jit_solution(1936622645766868482)
XLA Ops:
  6.3 6.5 %copy.184 = f32[32,256,64]{2,0,1:T(8,128)} copy(f32[32,256,64]{2,1,0:T(8,128)} %reshape.87) | data formatting | bytes 4194304 | tf_op jit(solution)/shard_map/reshape | solution.py:42
  17.8 6.5 %copy.185 = f32[32,256,64]{2,1,0:T(8,128)} copy(f32[32,256,64]{2,0,1:T(8,128)} %bitcast.78) | data formatting | bytes 4194304 | tf_op jit(solution)/shard_map/jit(_take)/gather | solution.py:42
  29.4 57.5 %all_to_all.18 = f32[32,128,128]{2,0,1:T(8,128)S(1)} all-to-all(f32[32,128,128]{2,0,1:T(8,128)S(1)} %copy.186), channel_id=1, replica_groups=mesh['pair'=32,'row'=16] {'pair'}, dimensions={1} | all-to-all | bytes 4194304 | tf_op jit(solution)/shard_map/all_to_all | solution.py:44
  98.4 6.6 %collective-permute-done.1 = f32[4,128,128]{1,2,0:T(8,128)S(1)} collective-permute-done((f32[4,128,128]{1,2,0:T(8,128)S(1)}, f32[4,128,128]{1,2,0:T(8,128)S(1)}, u32[]{:S(2)}, u32[]{:S(2)}) %collective-permute-start.1) | collective-permute-done | bytes 262176 | tf_op jit(solution)/shard_map/ppermute | solution.py:53
  111.2 11.6 %collective-permute-done.2 = f32[4,128,128]{1,2,0:T(8,128)S(1)} collective-permute-done((f32[4,128,128]{1,2,0:T(8,128)S(1)}, f32[4,128,128]{1,2,0:T(8,128)S(1)}, u32[]{:S(2)}, u32[]{:S(2)}) %collective-permute-start.2) | collective-permute-done | bytes 262176 | tf_op jit(solution)/shard_map/ppermute | solution.py:53
  122.8 8.5 %collective-permute-start.3 = (f32[4,128,128]{1,2,0:T(8,128)S(1)}, f32[4,128,128]{1,2,0:T(8,128)S(1)}, u32[]{:S(2)}, u32[]{:S(2)}) collective-permute-start(f32[4,128,128]{1,2,0:T(8,128)S(1)} %add.125), channel_id=1, source_target_pairs={{0,8},{1,9},{2,10},{3,11},{4,12},{5,13},{6,14},{7,15},{8,0},{9,1},... | collective-permute-start | bytes 786440 | tf_op jit(solution)/shard_map/ppermute | solution.py:53
  131.3 11.2 %collective-permute-done.3 = f32[4,128,128]{1,2,0:T(8,128)S(1)} collective-permute-done((f32[4,128,128]{1,2,0:T(8,128)S(1)}, f32[4,128,128]{1,2,0:T(8,128)S(1)}, u32[]{:S(2)}, u32[]{:S(2)}) %collective-permute-start.3) | collective-permute-done | bytes 262176 | tf_op jit(solution)/shard_map/ppermute | solution.py:53
  143.2 7.5 %copy.191 = f32[4,128,128]{0,2,1:T(8,128)} copy(f32[4,128,128]{1,2,0:T(8,128)S(1)} %get-tuple-element.18) | data formatting | bytes 524288 | tf_op jit(solution)/shard_map/add | solution.py:53
  154.1 46.9 %custom-call.18 = f32[4,128,128]{2,1,0:T(8,128)S(1)} custom-call(f32[4,128,128]{2,1,0:T(8,128)S(1)} %fusion.14), custom_call_target="Cholesky" | custom-call | tf_op jit(solution)/shard_map/vmap(jit(cholesky))/cholesky | solution.py:26
  201.3 39.7 %custom-call.19 = f32[4,1,128,128]{2,3,1,0:T(8,128)S(1)} custom-call(f32[4,1,128,128]{3,2,1,0:T(8,128)S(1)} %select_bitcast_fusion.2), custom_call_target="InvertDiagBlocksLowerTriangular" | custom-call | tf_op jit(solution)/shard_map/vmap(jit(_cho_solve))/triangular_solve | solution.py:27
  252.9 8.3 %collective-permute-done.5 = f32[4,128,128]{1,2,0:T(8,128)S(1)} collective-permute-done((f32[4,128,128]{1,2,0:T(8,128)S(1)}, f32[4,128,128]{1,2,0:T(8,128)S(1)}, u32[]{:S(2)}, u32[]{:S(2)}) %collective-permute-start.5) | collective-permute-done | bytes 262176 | tf_op jit(solution)/shard_map/ppermute | solution.py:53
  266.2 11.6 %collective-permute-done.6 = f32[4,128,128]{1,2,0:T(8,128)S(1)} collective-permute-done((f32[4,128,128]{1,2,0:T(8,128)S(1)}, f32[4,128,128]{1,2,0:T(8,128)S(1)}, u32[]{:S(2)}, u32[]{:S(2)}) %collective-permute-start.6) | collective-permute-done | bytes 262176 | tf_op jit(solution)/shard_map/ppermute | solution.py:53
  282.6 13.5 %collective-permute-done.7 = f32[4,128,128]{1,2,0:T(8,128)S(1)} collective-permute-done((f32[4,128,128]{1,2,0:T(8,128)S(1)}, f32[4,128,128]{1,2,0:T(8,128)S(1)}, u32[]{:S(2)}, u32[]{:S(2)}) %collective-permute-start.7) | collective-permute-done | bytes 262176 | tf_op jit(solution)/shard_map/ppermute | solution.py:53
  296.1 7.7 %copy.202 = f32[4,128,128]{0,2,1:T(8,128)} copy(f32[4,128,128]{1,2,0:T(8,128)S(1)} %add.133) | data formatting | bytes 524288 | tf_op jit(solution)/shard_map/add | solution.py:53
  307.2 46.9 %custom-call.20 = f32[4,128,128]{2,1,0:T(8,128)S(1)} custom-call(f32[4,128,128]{2,1,0:T(8,128)S(1)} %fusion.9), custom_call_target="Cholesky" | custom-call | tf_op jit(solution)/shard_map/vmap(jit(cholesky))/cholesky | solution.py:26
  354.4 39.5 %custom-call.21 = f32[4,1,128,128]{2,3,1,0:T(8,128)S(1)} custom-call(f32[4,1,128,128]{3,2,1,0:T(8,128)S(1)} %select_bitcast_fusion.1), custom_call_target="InvertDiagBlocksLowerTriangular" | custom-call | tf_op jit(solution)/shard_map/vmap(jit(_cho_solve))/triangular_solve | solution.py:27
  407.4 8.3 %collective-permute-done.9 = f32[4,128,128]{1,2,0:T(8,128)S(1)} collective-permute-done((f32[4,128,128]{1,2,0:T(8,128)S(1)}, f32[4,128,128]{1,2,0:T(8,128)S(1)}, u32[]{:S(2)}, u32[]{:S(2)}) %collective-permute-start.9) | collective-permute-done | bytes 262176 | tf_op jit(solution)/shard_map/ppermute | solution.py:53
  420.9 11.6 %collective-permute-done.10 = f32[4,128,128]{1,2,0:T(8,128)S(1)} collective-permute-done((f32[4,128,128]{1,2,0:T(8,128)S(1)}, f32[4,128,128]{1,2,0:T(8,128)S(1)}, u32[]{:S(2)}, u32[]{:S(2)}) %collective-permute-start.10) | collective-permute-done | bytes 262176 | tf_op jit(solution)/shard_map/ppermute | solution.py:53
  437.6 13.4 %collective-permute-done.11 = f32[4,128,128]{1,2,0:T(8,128)S(1)} collective-permute-done((f32[4,128,128]{1,2,0:T(8,128)S(1)}, f32[4,128,128]{1,2,0:T(8,128)S(1)}, u32[]{:S(2)}, u32[]{:S(2)}) %collective-permute-start.11) | collective-permute-done | bytes 262176 | tf_op jit(solution)/shard_map/ppermute | solution.py:53
  451.1 7.8 %copy.213 = f32[4,128,128]{0,2,1:T(8,128)} copy(f32[4,128,128]{1,2,0:T(8,128)S(1)} %add.140) | data formatting | bytes 524288 | tf_op jit(solution)/shard_map/add | solution.py:53
  462.2 46.9 %custom-call.22 = f32[4,128,128]{2,1,0:T(8,128)S(1)} custom-call(f32[4,128,128]{2,1,0:T(8,128)S(1)} %fusion.4), custom_call_target="Cholesky" | custom-call | tf_op jit(solution)/shard_map/vmap(jit(cholesky))/cholesky | solution.py:26
  509.4 39.6 %custom-call.23 = f32[4,1,128,128]{2,3,1,0:T(8,128)S(1)} custom-call(f32[4,1,128,128]{3,2,1,0:T(8,128)S(1)} %select_bitcast_fusion), custom_call_target="InvertDiagBlocksLowerTriangular" | custom-call | tf_op jit(solution)/shard_map/vmap(jit(_cho_solve))/triangular_solve | solution.py:27
  556.1 6.9 %collective-permute-start.13 = (f32[1024,64]{0,1:T(8,128)}, f32[1024,64]{0,1:T(8,128)}, u32[]{:S(2)}, u32[]{:S(2)}) collective-permute-start(f32[1024,64]{0,1:T(8,128)} %slice_bitcast_fusion), channel_id=1, source_target_pairs={{16,0},{32,16},{48,32},{64,48},{80,64},{96,80},{112,96},{128,112},... | collective-permute-start | bytes 786440 | tf_op jit(solution)/shard_map/ppermute | solution.py:13
  563.1 73.5 %all-reduce = (f32[]{:T(128)}, f32[]{:T(128)}) all-reduce(f32[]{:T(128)} %get-tuple-element.15, f32[]{:T(128)} %get-tuple-element.14), channel_id=1, replica_groups=mesh['pair'=32,'row'=16] {'pair'}, use_global_device_ids=true, to_apply=%region_3.6 | all-reduce | flops 2 | bytes 16 | tf_op jit(solution)/shard_map/psum | solution.py:58
  (105 shorter events, 101.7 us)
Async XLA Ops:
  90.7 3.4 collective-permute-start
  94.1 10.9 %collective-permute-start.1 = (f32[4,128,128]{1,2,0:T(8,128)S(1)}, f32[4,128,128]{1,2,0:T(8,128)S(1)}, u32[]{:S(2)}, u32[]{:S(2)}) collective-permute-start(f32[4,128,128]{1,2,0:T(8,128)S(1)} %add.123), channel_id=1, source_target_pairs={{0,2},{1,3},{2,0},{3,1},{4,6},{5,7},{6,4},{7,5},{8,10},{9,11},{10,... | collective-permute-start | bytes 786440 | tf_op jit(solution)/shard_map/ppermute | solution.py:53
  105.1 17.7 %collective-permute-start.2 = (f32[4,128,128]{1,2,0:T(8,128)S(1)}, f32[4,128,128]{1,2,0:T(8,128)S(1)}, u32[]{:S(2)}, u32[]{:S(2)}) collective-permute-start(f32[4,128,128]{1,2,0:T(8,128)S(1)} %add.124), channel_id=1, source_target_pairs={{0,4},{1,5},{2,6},{3,7},{4,0},{5,1},{6,2},{7,3},{8,12},{9,13},{10,... | collective-permute-start | bytes 786440 | tf_op jit(solution)/shard_map/ppermute | solution.py:53
  122.8 19.7 %collective-permute-start.3 = (f32[4,128,128]{1,2,0:T(8,128)S(1)}, f32[4,128,128]{1,2,0:T(8,128)S(1)}, u32[]{:S(2)}, u32[]{:S(2)}) collective-permute-start(f32[4,128,128]{1,2,0:T(8,128)S(1)} %add.125), channel_id=1, source_target_pairs={{0,8},{1,9},{2,10},{3,11},{4,12},{5,13},{6,14},{7,15},{8,0},{9,1},... | collective-permute-start | bytes 786440 | tf_op jit(solution)/shard_map/ppermute | solution.py:53
  244.0 3.6 copy-start
  247.5 3.4 collective-permute-start.4
  251.0 10.2 %collective-permute-start.5 = (f32[4,128,128]{1,2,0:T(8,128)S(1)}, f32[4,128,128]{1,2,0:T(8,128)S(1)}, u32[]{:S(2)}, u32[]{:S(2)}) collective-permute-start(f32[4,128,128]{1,2,0:T(8,128)S(1)} %add.130), channel_id=1, source_target_pairs={{0,2},{1,3},{2,0},{3,1},{4,6},{5,7},{6,4},{7,5},{8,10},{9,11},{10,... | collective-permute-start | bytes 786440 | tf_op jit(solution)/shard_map/ppermute | solution.py:53
  261.3 16.5 %collective-permute-start.6 = (f32[4,128,128]{1,2,0:T(8,128)S(1)}, f32[4,128,128]{1,2,0:T(8,128)S(1)}, u32[]{:S(2)}, u32[]{:S(2)}) collective-permute-start(f32[4,128,128]{1,2,0:T(8,128)S(1)} %add.131), channel_id=1, source_target_pairs={{0,4},{1,5},{2,6},{3,7},{4,0},{5,1},{6,2},{7,3},{8,12},{9,13},{10,... | collective-permute-start | bytes 786440 | tf_op jit(solution)/shard_map/ppermute | solution.py:53
  277.8 18.2 %collective-permute-start.7 = (f32[4,128,128]{1,2,0:T(8,128)S(1)}, f32[4,128,128]{1,2,0:T(8,128)S(1)}, u32[]{:S(2)}, u32[]{:S(2)}) collective-permute-start(f32[4,128,128]{1,2,0:T(8,128)S(1)} %add.132), channel_id=1, source_target_pairs={{0,8},{1,9},{2,10},{3,11},{4,12},{5,13},{6,14},{7,15},{8,0},{9,1},... | collective-permute-start | bytes 786440 | tf_op jit(solution)/shard_map/ppermute | solution.py:53
  402.0 3.4 collective-permute-start.8
  405.5 10.2 %collective-permute-start.9 = (f32[4,128,128]{1,2,0:T(8,128)S(1)}, f32[4,128,128]{1,2,0:T(8,128)S(1)}, u32[]{:S(2)}, u32[]{:S(2)}) collective-permute-start(f32[4,128,128]{1,2,0:T(8,128)S(1)} %add.137), channel_id=1, source_target_pairs={{0,2},{1,3},{2,0},{3,1},{4,6},{5,7},{6,4},{7,5},{8,10},{9,11},{10,... | collective-permute-start | bytes 786440 | tf_op jit(solution)/shard_map/ppermute | solution.py:53
  415.8 16.8 %collective-permute-start.10 = (f32[4,128,128]{1,2,0:T(8,128)S(1)}, f32[4,128,128]{1,2,0:T(8,128)S(1)}, u32[]{:S(2)}, u32[]{:S(2)}) collective-permute-start(f32[4,128,128]{1,2,0:T(8,128)S(1)} %add.138), channel_id=1, source_target_pairs={{0,4},{1,5},{2,6},{3,7},{4,0},{5,1},{6,2},{7,3},{8,12},{9,13},{10,... | collective-permute-start | bytes 786440 | tf_op jit(solution)/shard_map/ppermute | solution.py:53
  432.6 18.4 %collective-permute-start.11 = (f32[4,128,128]{1,2,0:T(8,128)S(1)}, f32[4,128,128]{1,2,0:T(8,128)S(1)}, u32[]{:S(2)}, u32[]{:S(2)}) collective-permute-start(f32[4,128,128]{1,2,0:T(8,128)S(1)} %add.139), channel_id=1, source_target_pairs={{0,8},{1,9},{2,10},{3,11},{4,12},{5,13},{6,14},{7,15},{8,0},{9,1},... | collective-permute-start | bytes 786440 | tf_op jit(solution)/shard_map/ppermute | solution.py:53
  552.0 1.7 copy-start.1
  553.8 85.5 %collective-permute-start.12 = (f32[1024,64]{0,1:T(8,128)}, f32[1024,64]{0,1:T(8,128)S(1)}, u32[]{:S(2)}, u32[]{:S(2)}) collective-permute-start(f32[1024,64]{0,1:T(8,128)} %slice_bitcast_fusion.1), channel_id=1, source_target_pairs={{0,16},{16,32},{32,48},{48,64},{64,80},{80,96},{96,112},{112,128},... | collective-permute-start | bytes 786440 | tf_op jit(solution)/shard_map/ppermute | solution.py:13
  556.1 83.2 %copy-start.2 = (f32[4,1024,128]{1,2,0:T(8,128)S(1)}, f32[4,1024,128]{1,2,0:T(8,128)}, u32[]{:S(2)}) copy-start(f32[4,1024,128]{1,2,0:T(8,128)} %copy-done.1) | copy-start | bytes 6291460
  556.1 83.1 %collective-permute-start.13 = (f32[1024,64]{0,1:T(8,128)}, f32[1024,64]{0,1:T(8,128)}, u32[]{:S(2)}, u32[]{:S(2)}) collective-permute-start(f32[1024,64]{0,1:T(8,128)} %slice_bitcast_fusion), channel_id=1, source_target_pairs={{16,0},{32,16},{48,32},{64,48},{80,64},{96,80},{112,96},{128,112},... | collective-permute-start | bytes 786440 | tf_op jit(solution)/shard_map/ppermute | solution.py:13
